TPU v7x, 32 devices: a whole 2x2x4 slice. The times are simulated.
32 devices in a mesh: seq: 8 (over z, y), head: 4 (over x, core).
Axes of the slice: x: 2, y: 2, z: 4, core: 2. Of those that a mesh axis runs over, the one named last changes fastest.
Arguments:
- queries: bfloat16 [2, 64, 64, 128], P(None, 'head'), may hold values from -9 to 9
- cache_keys: bfloat16 [2, 8, 8192, 128], P(None, 'head', 'seq'), may hold values from -10 to 10
- cache_values: bfloat16 [2, 8, 8192, 128], P(None, 'head', 'seq'), may hold values from -6 to 6
- new_keys: bfloat16 [2, 8, 64, 128], P(None, 'head'), may hold values from -20 to 20
- new_values: bfloat16 [2, 8, 64, 128], P(None, 'head'), may hold values from -6 to 6
- parents: int32 [2, 64], replicated, may hold values from 0 to 62, as said below
- path: int32 [2, 6], replicated, may hold values from 0 to 63, as said below
- lengths: int32 [2], replicated, may hold values from 2048 to 8192, as said below
- draft_tokens: int32 [2, 64], replicated, may hold values from 0 to 65535
- residual: bfloat16 [2, 64, 8192], P(None, None, 'seq'), may hold values from -8 to 8
- out_weight: bfloat16 [8192, 8192], P('head', 'seq'), may hold values from -0.0625 to 0.0625
- norm_gain: bfloat16 [8192], P('seq'), may hold values from 0.5 to 1.5
- vocab_weight: bfloat16 [8192, 65536], P(None, ('seq', 'head')), may hold values from -3 to 3
Outputs:
- path_logits: float32 [2, 6, 65536], P(None, None, ('seq', 'head'))
- draft_logprob: float32 [2, 64], replicated
Inputs may be any that keep to these rules, and one draw needn't show every extreme that they name: parents[b, 0] is 0; for every other node n, parents[b, n] is a smaller node number. path[b] lists 6 different nodes: node 0 first, and each later entry is a child (by parents) of the entry before it. `lengths`: at least one sequence uses all 8192 cache positions.
All inputs are finite; a program needn't handle non-finite values.
Results may differ from a plain program's by a relative error of at most 0.006.
Values may be sent and summed in bfloat16 or wider, within the bound.
A program may use at most 128 MiB of HBM per device.

v0:
```python
import jax
import jax.numpy as jnp
from jax import lax
from jax.sharding import PartitionSpec as P

D = 8192


lowest = -1e30
epsilon = 1e-05


def ancestors(parents):
    node_count = parents.shape[-1]
    node_ids = jnp.arange(node_count, dtype=jnp.int32)
    linked = (parents[..., :, None] == node_ids[None, None, :]).astype(jnp.float32)
    reached = jnp.maximum(linked, jnp.eye(node_count, dtype=jnp.float32)[None])
    for _ in range(node_count.bit_length()):
        reached = jnp.minimum(jnp.einsum("bij,bjk->bik", reached, reached), 1.0)
    return reached > 0.5


def block_state(scores, visible, values):
    masked = jnp.where(visible, scores, lowest)
    block_max = jnp.max(masked, axis=-1)
    weights = jnp.where(visible, jnp.exp(masked - block_max[..., None]), 0.0).astype(jnp.bfloat16)
    block_total = jnp.sum(weights.astype(jnp.float32), axis=-1)
    block_out = jnp.einsum("kqc,kcd->kqd", weights, values, preferred_element_type=jnp.float32)
    return (block_max, block_total, block_out)


def join_states(earlier, later):
    summit = jnp.maximum(earlier[0], later[0])
    damp_early = jnp.exp(earlier[0] - summit)
    damp_later = jnp.exp(later[0] - summit)
    total_joined = earlier[1] * damp_early + later[1] * damp_later
    out_joined = earlier[2] * damp_early[..., None] + later[2] * damp_later[..., None]
    return (summit, total_joined, out_joined)


def on_device(
    queries,
    cache_keys,
    cache_values,
    new_keys,
    new_values,
    parents,
    path,
    lengths,
    draft_tokens,
    residual,
    out_weight,
    norm_gain,
    vocab_weight,
):
    batch_size, heads_local, node_count, head_dim = queries.shape
    kv_local = cache_keys.shape[1]
    span_local = cache_keys.shape[2]
    group_size = heads_local // kv_local
    score_scale = head_dim ** (-0.5)
    seq_index = lax.axis_index("seq")
    reached = ancestors(parents)
    is_owner = seq_index == 0
    offsets = seq_index * span_local + jnp.arange(span_local, dtype=jnp.int32)

    def per_sequence(entries):
        query_block, key_block, value_block, tree_keys, tree_values, reach_row, length = entries
        grouped = query_block.reshape(kv_local, group_size * node_count, head_dim)
        scores = (
            jnp.einsum("kqd,kcd->kqc", grouped, key_block, preferred_element_type=jnp.float32)
            * score_scale
        )
        live_keys = (offsets < length)[None, None, :]
        cache_state = block_state(scores, live_keys, value_block)
        tree_scores = (
            jnp.einsum("kqd,kcd->kqc", grouped, tree_keys, preferred_element_type=jnp.float32)
            * score_scale
        )
        tree_seen = jnp.logical_and(jnp.tile(reach_row, (group_size, 1))[None], is_owner)
        tree_state = block_state(tree_scores, tree_seen, tree_values)
        return join_states(cache_state, tree_state)

    maxima, totals, outputs = lax.map(
        per_sequence, (queries, cache_keys, cache_values, new_keys, new_values, reached, lengths)
    )
    weight_heads = out_weight.reshape(heads_local, head_dim, -1)
    highest = lax.pmax(maxima, "seq")
    factors = jnp.exp(maxima - highest)
    scaled = (outputs * factors[..., None]).reshape(batch_size, heads_local, node_count, head_dim)
    summed = (totals * factors).reshape(batch_size, heads_local, node_count)
    share_out, share_total = (
        lax.psum_scatter(scaled, "seq", scatter_dimension=2, tiled=True),
        lax.psum_scatter(summed, "seq", scatter_dimension=2, tiled=True),
    )
    attention = (share_out / share_total[..., None]).astype(jnp.bfloat16)
    projected = jnp.einsum(
        "bhnd,hdc->bnc",
        lax.all_gather(attention, "seq", axis=2, tiled=True),
        weight_heads,
        preferred_element_type=jnp.float32,
    )
    vocab_local = vocab_weight.shape[1]
    projected = lax.psum(projected, "head")
    stream = residual.astype(jnp.float32) + projected
    gain_part = norm_gain.astype(jnp.float32)
    square_sum = lax.psum(jnp.sum(stream * stream, axis=-1), "seq")
    normed = (stream * lax.rsqrt(square_sum / D + epsilon)[..., None] * gain_part).astype(
        jnp.bfloat16
    )
    portion = lax.all_gather(normed, "seq", axis=2, tiled=True)
    flat_part = portion.reshape(batch_size * node_count, portion.shape[2])
    logits = jnp.dot(flat_part, vocab_weight, preferred_element_type=jnp.float32)
    logits = logits.reshape(batch_size, node_count, vocab_local)
    vocab_first = lax.axis_index(("seq", "head")) * vocab_local
    vocab_ids = jnp.arange(vocab_local, dtype=jnp.int32) + vocab_first
    picked = jnp.sum(jnp.where(draft_tokens[..., None] == vocab_ids, logits, 0.0), axis=-1)
    local_max = jnp.max(logits, axis=-1)
    vocab_top = lax.pmax(local_max, ("seq", "head"))
    local_sum = jnp.sum(jnp.exp(logits - vocab_top[..., None]), axis=-1)
    exp_sums, picked = lax.psum((local_sum, picked), ("seq", "head"))
    draft_logprob = picked - (vocab_top + jnp.log(exp_sums))
    path_logits = jnp.take_along_axis(logits, path[:, :, None], axis=1)
    return (path_logits, draft_logprob)


def solution(mesh):
    placed = (
        P(None, "head", None, None),
        P(None, "head", "seq", None),
        P(None, "head", "seq", None),
        P(None, "head", None, None),
        P(None, "head", None, None),
        P(),
        P(),
        P(),
        P(),
        P(None, None, "seq"),
        P("head", "seq"),
        P("seq"),
        P(None, ("seq", "head")),
    )
    return jax.shard_map(
        on_device,
        mesh=mesh,
        in_specs=placed,
        out_specs=(P(None, None, ("seq", "head")), P()),
        check_vma=False,
    )
```

profile of v0, /device:TPU:0, one launch (start us, length us, event | category | flops | bytes accessed | tf_op | source)
XLA Modules:
  0.0 349.0 jit_solution(16134530394701500435)
XLA Ops:
  7.2 0.0 reduce-scatter.2.cloned.1.call-start
  7.3 1.0 convolution_minimum_fusion.6
  8.2 0.3 convolution_minimum_fusion.4
  8.5 0.3 convolution_minimum_fusion.2
  8.8 0.3 fusion.30
  9.1 0.0 copy-start.6
  9.1 17.6 %while.15 = (s32[]{:T(128)}, f32[2,2,512]{2,1,0:T(2,128)S(1)}, f32[2,2,512]{2,1,0:T(2,128)S(1)}, f32[2,2,512,128]{3,2,1,0:T(8,128)S(1)}, s32[2]{0:T(128)}, /*ind...) while((s32[]{:T(128)}, f32[2,2,512]{2,1,0:T(2,128)S(1)}, ...), condition=%wide.region_5.6_spmd.clone, body=%wide.region_0.5_spmd.clone.sunk | while | flops 587279360 | bytes 21873904 | solution.py:83
  9.1 1.0 constant_dynamic-slice_fusion.5
  10.1 0.1 copy.30
  10.3 0.2 and.42
  10.4 1.0 fusion.69
  11.4 0.1 convert_reduce_fusion.4
  11.5 1.2 dynamic_slice.68
  12.7 0.6 add_compare_fusion.2
  13.3 0.0 copy-start.1
  13.3 0.0 copy-start.5
  13.3 2.0 fusion.70
  15.3 1.2 convert_reduce_fusion.5
  16.5 0.3 convolution_multiply_fusion.4
  16.9 1.1 fusion.73
  17.9 1.0 constant_dynamic-slice_fusion.5
  18.9 0.1 copy.30
  19.1 0.2 and.42
  19.2 1.0 fusion.69
  20.2 0.1 convert_reduce_fusion.4
  20.3 1.2 dynamic_slice.68
  21.5 0.6 add_compare_fusion.2
  22.1 0.0 copy-start.1
  22.1 2.0 fusion.70
  24.1 1.2 convert_reduce_fusion.5
  25.3 0.3 convolution_multiply_fusion.4
  25.7 1.1 fusion.73
  26.7 23.4 %pmax.14 = f32[2,2,512]{2,1,0:T(2,128)S(1)} all-reduce(f32[2,2,512]{2,1,0:T(2,128)S(1)} %get-tuple-element.72), channel_id=1, replica_groups=mesh['seq'=8,'head'=4] {'seq'}, use_global_device_ids=true, to_apply=%region_6.7 | all-reduce | flops 2048 | bytes 16384 | tf_op jit(solution)/shard_map/pmax | solution.py:87
  50.2 1.3 broadcast_multiply_fusion
  51.5 0.0 reduce-scatter.2.cloned.1.call-update
  51.5 0.0 all-reduce.4.cloned.1.call-start
  51.6 0.1 reshape.133
  51.7 0.1 copy.24
  51.8 0.6 dynamic-slice
  53.0 33.4 %all-reduce = f32[2,16,64]{1,0,2:T(2,128)S(1)} all-reduce(f32[2,16,64]{1,0,2:T(2,128)S(1)} %copy.24), channel_id=3, replica_groups=mesh['seq'=8,'head'=4] {'seq'}, use_global_device_ids=true, to_apply=%region_8.9.clone | all-reduce | flops 2048 | bytes 16384
  86.4 0.0 copy-start.2
  86.4 0.0 copy-start
  86.5 0.1 copy.25
  86.6 27.2 %reduce-scatter.2.cloned.1.call-done = f32[2,16,8,128]{3,2,1,0:T(8,128)} async-done(((f32[2,16,64,128]{3,2,1,0:T(8,128)}), f32[2,16,8,128]{3,2,1,0:T(8,128)}) %reduce-scatter.2.cloned.1.call-update) | async-done | bytes 131088 | tf_op jit(solution)/shard_map/reduce_scatter | solution.py:92
  113.7 1.0 divide_convert_fusion
  114.7 27.1 %all_gather.6 = bf16[2,16,64,128]{3,2,1,0:T(8,128)(2,1)S(1)} all-gather(bf16[2,16,8,128]{3,2,1,0:T(8,128)(2,1)S(1)} %divide_convert_fusion), channel_id=1, replica_groups=mesh['seq'=8,'head'=4] {'seq'}, dimensions={2}, use_global_device_ids=true | all-gather | bytes 589824 | tf_op jit(solution)/shard_map/all_gather | solution.py:98
  141.9 3.8 %convolution_bitcast_fusion = f32[2,64,1024]{2,1,0:T(8,128)} fusion(bf16[2,16,64,128]{3,2,1,0:T(8,128)(2,1)S(1)} %all_gather.6, bf16[16,128,1024,1]{2,1,0,3:T(8,128)(2,1)} %bitcast.116), kind=kOutput, calls=%fused_computation.49 | convolution fusion | flops 536870912 | bytes 5242880 | tf_op jit(solution)/shard_map/bhnd,hdc->bnc/dot_general | solution.py:96
  145.7 0.0 all-reduce.4.cloned.1.call-update
  145.7 0.0 all-gather.2.cloned.1.call-start
  145.8 31.3 %all-reduce.4.cloned.1.call-done = f32[2,64,1024]{2,1,0:T(8,128)} async-done(((f32[2,64,1024]{2,1,0:T(8,128)}), f32[2,64,1024]{2,1,0:T(8,128)}) %all-reduce.4.cloned.1.call-update) | async-done | bytes 524304 | tf_op jit(solution)/shard_map/psum | solution.py:103
  177.1 1.2 multiply_reduce_fusion
  178.3 21.4 %psum.29 = f32[2,64]{1,0:T(2,128)S(1)} all-reduce(f32[2,64]{1,0:T(2,128)S(1)} %multiply_reduce_fusion), channel_id=1, replica_groups=mesh['seq'=8,'head'=4] {'seq'}, use_global_device_ids=true, to_apply=%region_11.12 | all-reduce | flops 128 | bytes 1024 | tf_op jit(solution)/shard_map/psum | solution.py:106
  199.7 1.9 multiply_convert_fusion
  201.5 0.0 all-gather.2.cloned.1.call-update
  201.6 0.1 reshape.135
  201.7 45.5 %all-gather.2.cloned.1.call-done = bf16[2,64,8192]{2,1,0:T(8,128)(2,1)} async-done(((bf16[2,64,1024]{2,1,0:T(8,128)(2,1)}), bf16[2,64,8192]{2,1,0:T(8,128)(2,1)}) %all-gather.2.cloned.1.call-update) | async-done | bytes 2097168 | tf_op jit(solution)/shard_map/all_gather | solution.py:110
  247.2 13.6 %fusion.44 = (f32[2,64]{1,0:T(2,128)S(1)}, f32[2,64,2048]{2,1,0:T(8,128)S(1)}) fusion(bf16[2,64,8192]{2,1,0:T(8,128)(2,1)} %all-gather.2.cloned.1.call-done, bf16[8192,2048]{1,0:T(8,128)(2,1)} %param.27), kind=kOutput, calls=%fused_computation.89 | convolution fusion | flops 4295229440 | bytes 36700672 | tf_op jit(solution)/shard_map/dot_general | solution.py:112
  260.8 0.7 gather_fusion
  261.6 0.1 broadcast_select_fusion
  261.7 0.7 copy.26
  262.4 39.2 %pmax.15 = f32[2,64]{1,0:T(2,128)S(1)} all-reduce(f32[2,64]{1,0:T(2,128)S(1)} %get-tuple-element.201), channel_id=1, replica_groups=mesh['seq'=8,'head'=4] {'seq','head'}, use_global_device_ids=true, to_apply=%region_15.16 | all-reduce | flops 128 | bytes 1024 | tf_op jit(solution)/shard_map/pmax | solution.py:118
  301.5 0.4 exponential_reduce_fusion
  301.9 40.0 %all-reduce.1 = (f32[2,64]{1,0:T(2,128)S(1)}, f32[2,64]{1,0:T(2,128)S(1)}) all-reduce(f32[2,64]{1,0:T(2,128)S(1)} %get-tuple-element.162, f32[2,64]{1,0:T(2,128)S(1)} %get-tuple-element.161), channel_id=1, replica_groups=mesh['seq'=8,'head'=4] {'seq','head'}, use_global_device_ids=true, to_apply=%region_13.14 | all-reduce | flops 256 | bytes 2048 | tf_op jit(solution)/shard_map/psum | solution.py:120
  341.9 0.6 add_subtract_fusion
  (34 shorter events, 0.3 us)
Async XLA Ops:
  7.2 106.6 %reduce-scatter.2.cloned.1.call-start = ((), (), s32[]{:S(2)}) async-start(), calls=%async_computation.1 | async-start | bytes 1179648 | tf_op jit(solution)/shard_map/reduce_scatter | solution.py:92
  9.1 42.7 %copy-start.6 = (u32[32]{0:T(128)S(1)}, u32[32]{0:T(128)}, u32[]{:S(2)}) copy-start(u32[32]{0:T(128)} %constant.93) | copy-start | bytes 388
  13.3 3.2 copy-start.1
  13.3 3.5 %copy-start.5 = (bf16[2,2,1024,128]{3,2,1,0:T(8,128)(2,1)S(1)}, bf16[2,2,1024,128]{3,2,1,0:T(8,128)(2,1)}, u32[]{:S(2)}) copy-start(bf16[2,2,1024,128]{3,2,1,0:T(8,128)(2,1)} %get-tuple-element.336) | copy-start | bytes 3145732 | tf_op jit(solution)/shard_map/while
  22.1 3.2 copy-start.1
  22.1 3.5 %copy-start.5 = (bf16[2,2,1024,128]{3,2,1,0:T(8,128)(2,1)S(1)}, bf16[2,2,1024,128]{3,2,1,0:T(8,128)(2,1)}, u32[]{:S(2)}) copy-start(bf16[2,2,1024,128]{3,2,1,0:T(8,128)(2,1)} %get-tuple-element.336) | copy-start | bytes 3145732 | tf_op jit(solution)/shard_map/while
  51.5 125.6 %all-reduce.4.cloned.1.call-start = ((), (), s32[]{:S(2)}) async-start(), calls=%async_computation.2 | async-start | bytes 1048576 | tf_op jit(solution)/shard_map/psum | solution.py:103
  86.4 59.3 %copy-start.2 = (bf16[1024]{0:T(1024)(128)(2,1)S(1)}, bf16[1024]{0:T(1024)(128)(2,1)}, u32[]{:S(2)}) copy-start(bf16[1024]{0:T(1024)(128)(2,1)} %param.26) | copy-start | bytes 6148
  86.4 90.7 %copy-start = (bf16[2,64,1024]{2,1,0:T(8,128)(2,1)S(1)}, bf16[2,64,1024]{2,1,0:T(8,128)(2,1)}, u32[]{:S(2)}) copy-start(bf16[2,64,1024]{2,1,0:T(8,128)(2,1)} %param.24) | copy-start | bytes 786436
  141.9 59.7 %copy-start.3 = (s32[2,6]{1,0:T(2,128)S(1)}, s32[2,6]{1,0:T(2,128)}, u32[]{:S(2)}) copy-start(s32[2,6]{1,0:T(2,128)} %param.21) | copy-start | bytes 148
  145.7 101.5 %all-gather.2.cloned.1.call-start = ((), (), s32[]{:S(2)}) async-start(), calls=%async_computation.3 | async-start | bytes 2359296 | tf_op jit(solution)/shard_map/all_gather | solution.py:110
  201.7 99.9 %copy-start.4 = (s32[2,64]{1,0:T(2,128)S(1)}, s32[2,64]{1,0:T(2,128)}, u32[]{:S(2)}) copy-start(s32[2,64]{1,0:T(2,128)} %param.23) | copy-start | bytes 1540
Sparse Core Ops, SparseCore 0:
  51.6 62.0 reduce-scatter.1
  145.8 31.2 all-reduce.3
  201.7 45.4 all-gather.1
where the time goes:
time: 350 us; the launch traced here: 349 us
  blocking collectives  184 us (53%)
  waiting for transfers between devices  104 us (30%)
  matrix products  27.8 us (8%)
  between operations  14.6 us (4%)
  other arithmetic  10.2 us (3%)
  local copies, waits for them, and re-layouts  7.47 us (2%)
    all_gather x1, waiting for transfers between devices, on_device(): portion = lax.all_gather(normed, 'seq', axis=2, tiled=True)  45.5 us
    psum x1, blocking collectives, on_device(): exp_sums, picked = lax.psum((local_sum, picked), ('seq', 'head'))  40 us
    pmax x1, blocking collectives, on_device(): vocab_top = lax.pmax(local_max, ('seq', 'head'))  39.2 us
    unnamed x1, blocking collectives  33.4 us
    psum x1, waiting for transfers between devices, on_device(): projected = lax.psum(projected, 'head')  31.3 us
    reduce_scatter x1, waiting for transfers between devices, on_device(): lax.psum_scatter(scaled, 'seq', scatter_dimension=2, tiled=True)  27.2 us
    all_gather x1, blocking collectives, on_device(): lax.all_gather(attention, 'seq', axis=2, tiled=True)  27.1 us
    pmax x1, blocking collectives, on_device(): highest = lax.pmax(maxima, 'seq')  23.4 us
  transfers between devices with their start and end apart: 3, of which 3 were waited for; matrix products, arithmetic and copies ran while one was open for 0% of the time, Pallas kernels for 0%

commit v1 on v0

v1 whole, which is shorter than its diff:
```python
import functools
import math

import jax
import jax.numpy as jnp
from jax import lax
from jax.experimental import pallas as pl
from jax.experimental.pallas import tpu as pltpu
from jax.sharding import PartitionSpec as P

lowest = -1e30
epsilon = 1e-05
MESH = pl.DeviceIdType.MESH
f32 = jnp.float32
bf16 = jnp.bfloat16


def kernel(
    S, H, B, N, D,
    len_ref, path_ref, par_ref, draft_ref, gain_ref,
    q_hbm, k_hbm, v_hbm, nk_hbm, nv_hbm, res_hbm, ow_hbm, vw_hbm,
    path_out, logp_out,
    q, k, v, res, ow, vw, reach,
    o_send, ml_send, o_recv, ml_recv, a_send, x_att, p_send, p_recv, g, acc,
    ss_send, ss_r1, ss_mid, ss_r2, st_send, st_r1, st_mid, st_r2,
    load_sem, vw_sem,
    o_ss, o_rs, ml_ss, ml_rs, a_ss, a_rs, p_ss, p_rs, g_ss, g_rs,
    s1_ss, s1_rs, s2_ss, s2_rs, t1_ss, t1_rs, t2_ss, t2_rs,
):
    s = lax.axis_index("seq")
    h = lax.axis_index("head")
    R, HD = q.shape[1], q.shape[2]
    BK, keys = k.shape[0], k_hbm.shape[1]
    parts = S // BK
    rows = B * N
    HR = rows // H
    DL = ow.shape[1]
    VL = vw.shape[1]
    heads_chunk = R // N
    group = S // B

    def seq_peer(i):
        return lax.rem(s + i, S)

    def head_peer(i):
        return lax.rem(h + i, H)

    loads = [
        (q_hbm, q),
        (k_hbm, k.at[:, pl.ds(0, keys)]),
        (nk_hbm, k.at[:, pl.ds(keys, N)]),
        (v_hbm, v.at[:, pl.ds(0, keys)]),
        (nv_hbm, v.at[:, pl.ds(keys, N)]),
        (res_hbm, res),
        (ow_hbm, ow),
    ]
    loads = [
        pltpu.make_async_copy(src, dst, load_sem.at[i]) for i, (src, dst) in enumerate(loads)
    ]
    for c in loads:
        c.start()

    barrier = pltpu.get_barrier_semaphore()
    for i in range(1, S):
        pl.semaphore_signal(barrier, inc=1, device_id=(seq_peer(i), h), device_id_type=MESH)
    for i in range(1, H):
        pl.semaphore_signal(barrier, inc=1, device_id=(s, head_peer(i)), device_id_type=MESH)

    Z = S // 2
    y = lax.rem(s, 2)
    z = s // 2
    order = []
    for i in range(Z):
        zi = lax.rem(z + i, Z)
        order.append(zi * 2 + y)
        order.append(zi * 2 + (1 - y))

    def slab(idx):
        return pl.ds(pl.multiple_of(idx * DL, DL), DL)

    def vw_copy(n):
        return pltpu.make_async_copy(
            vw_hbm.at[slab(order[n])], vw.at[slab(order[n])], vw_sem.at[n]
        )

    for n in range(S):
        vw_copy(n).start()

    rid = lax.broadcasted_iota(jnp.int32, (N, N), 0)
    cid = lax.broadcasted_iota(jnp.int32, (N, N), 1)
    for b in range(B):
        link = jnp.logical_or(par_ref[b : b + 1, :] == rid, rid == cid)
        r = jnp.where(link, 1.0, 0.0)
        for _ in range(N.bit_length() - 1):
            rb = r.astype(bf16)
            r = jnp.minimum(jnp.dot(rb, rb, preferred_element_type=f32), 1.0)
        reach[b] = jnp.concatenate([r] * heads_chunk, axis=1)

    for c in loads[:5]:
        c.wait()

    scale = math.log2(math.e) * HD**-0.5
    key_id = lax.broadcasted_iota(jnp.int32, (keys, R), 0) + s * keys
    owner = s == 0

    def chunk(t):
        bk = t // parts
        b = t // group
        kk = k[bk]
        vv = v[bk]
        length = len_ref[0]
        for i in range(1, B):
            length = jnp.where(b == i, len_ref[i], length)
        score = lax.dot_general(kk, q[t], (((1,), (1,)), ((), ())), preferred_element_type=f32)
        cache = jnp.where(key_id < length, score[:keys] * scale, lowest)
        tree_seen = jnp.where(owner, reach[b], 0.0) > 0.5
        tree = jnp.where(tree_seen, score[keys:] * scale, lowest)
        top = jnp.maximum(
            jnp.max(cache, axis=0, keepdims=True), jnp.max(tree, axis=0, keepdims=True)
        )
        top = jnp.maximum(top, 0.1 * lowest)
        wc = jnp.exp2(cache - top)
        wt = jnp.exp2(tree - top)
        total = jnp.sum(wc, axis=0, keepdims=True) + jnp.sum(wt, axis=0, keepdims=True)
        w = jnp.concatenate([wc.astype(bf16), wt.astype(bf16)], axis=0)
        out = lax.dot_general(vv, w, (((0,), (0,)), ((), ())), preferred_element_type=f32)
        ml = jnp.concatenate(
            [jnp.broadcast_to(top, (4, R)), jnp.broadcast_to(total, (4, R))], axis=0
        )
        return out.astype(bf16), ml

    def remote(src, dst, ss, rs, dev):
        return pltpu.make_async_remote_copy(
            src_ref=src, dst_ref=dst, send_sem=ss, recv_sem=rs, device_id=dev, device_id_type=MESH
        )

    pl.semaphore_wait(barrier, S - 1 + H - 1)

    def send_chunk(i, carry):
        t = seq_peer(i)
        out, ml = chunk(t)
        o_send[t] = out
        ml_send[t] = ml
        remote(o_send.at[t], o_recv.at[s], o_ss.at[t], o_rs.at[s], (t, h)).start()
        remote(ml_send.at[t], ml_recv.at[s], ml_ss.at[t], ml_rs.at[s], (t, h)).start()
        return carry

    lax.fori_loop(1, S, send_chunk, 0)
    out, ml = chunk(s)
    o_recv[s] = out
    ml_recv[s] = ml

    for i in range(1, S):
        t = seq_peer(i)
        remote(o_send.at[t], o_recv.at[t], o_ss.at[t], o_rs.at[t], (t, h)).wait_recv()
        remote(ml_send.at[t], ml_recv.at[t], ml_ss.at[t], ml_rs.at[t], (t, h)).wait_recv()

    top = ml_recv[0, 0:1]
    for i in range(1, S):
        top = jnp.maximum(top, ml_recv[i, 0:1])
    total = jnp.zeros((1, R), f32)
    whole = jnp.zeros((HD, R), f32)
    for i in range(S):
        w = jnp.exp2(ml_recv[i, 0:1] - top)
        total += ml_recv[i, 4:5] * w
        whole += o_recv[i].astype(f32) * w
    att = jnp.transpose(whole / total).astype(bf16).reshape(heads_chunk, N, HD)

    def att_place(t):
        h0 = lax.rem(t, group) * heads_chunk
        return x_att.at[pl.ds(h0, heads_chunk), pl.ds(pl.multiple_of(t // group * N, N), N), :]

    a_send[...] = att
    for i in range(1, S):
        t = seq_peer(i)
        remote(a_send, att_place(s), a_ss.at[t], a_rs.at[s], (t, h)).start()
    x_att[
        pl.ds(lax.rem(s, group) * heads_chunk, heads_chunk),
        pl.ds(pl.multiple_of(s // group * N, N), N),
        :,
    ] = att
    loads[5].wait()
    loads[6].wait()
    for i in range(1, S):
        t = seq_peer(i)
        remote(a_send, att_place(t), a_ss.at[t], a_rs.at[t], (t, h)).wait_recv()

    lhs = jnp.concatenate([x_att[i] for i in range(x_att.shape[0])], axis=1)
    proj = jnp.dot(lhs, ow[...], preferred_element_type=f32)
    for j in range(H):
        p_send[j] = proj[j * HR : (j + 1) * HR].astype(bf16)
    for i in range(1, H):
        t = head_peer(i)
        remote(p_send.at[t], p_recv.at[h], p_ss.at[t], p_rs.at[h], (s, t)).start()
    my_rows = pl.ds(pl.multiple_of(h * HR, HR), HR)
    stream = res[my_rows, :].astype(f32) + p_send[h].astype(f32)
    for i in range(1, H):
        t = head_peer(i)
        remote(p_send.at[t], p_recv.at[t], p_ss.at[t], p_rs.at[t], (s, t)).wait_recv()
        stream += p_recv[t].astype(f32)
    g[s, my_rows, :] = (stream * gain_ref[...].astype(f32)).astype(bf16)

    def block(si, hi):
        return g.at[si, pl.ds(pl.multiple_of(hi * HR, HR), HR), :]

    sends = []

    def pass_on(si, hi, dev):
        c = remote(block(si, hi), block(si, hi), g_ss.at[len(sends)], g_rs.at[si * H + hi], dev)
        c.start()
        sends.append(c)

    def arrive(si, hi):
        remote(block(si, hi), block(si, hi), g_ss.at[0], g_rs.at[si * H + hi], (s, h)).wait_recv()

    HX = H // 2
    hx, hc = h // 2, lax.rem(h, 2)
    partner = hx * 2 + (1 - hc)
    far = [lax.rem(hx + i, HX) * 2 + hc for i in range(1, HX)]
    far_partner = [lax.rem(hx + i, HX) * 2 + (1 - hc) for i in range(1, HX)]
    y_dev = z * 2 + (1 - y)

    def first_hop(n):
        si = order[n]
        if n == 0:
            for i in range(1, Z):
                pass_on(si, h, (order[2 * i], h))
        else:
            arrive(si, h)
        if n % 2 == 0:
            pass_on(si, h, (y_dev, h))
        for t in far:
            pass_on(si, h, (s, t))
        pass_on(si, h, (s, partner))

    def second_hop(n):
        for t in far:
            arrive(order[n], t)
            pass_on(order[n], t, (s, partner))

    tiles = max(1, VL // 512)
    width = VL // tiles

    def product(n):
        arrive(order[n], partner)
        for t in far_partner:
            arrive(order[n], t)
        vw_copy(n).wait()
        left = g[order[n]]

        def tile(c, carry):
            cols = pl.ds(pl.multiple_of(c * width, width), width)
            part = jnp.dot(left, vw[slab(order[n]), cols], preferred_element_type=f32)
            acc[:, cols] = part if n == 0 else acc[:, cols] + part
            return carry

        lax.fori_loop(0, tiles, tile, 0)

    first_hop(0)

    eye = lax.broadcasted_iota(jnp.int32, (rows, rows), 0) == lax.broadcasted_iota(
        jnp.int32, (rows, rows), 1
    )

    def to_row(col):
        return jnp.sum(jnp.where(eye, col, 0.0), axis=0, keepdims=True)

    def to_col(row):
        return jnp.sum(jnp.where(eye, row, 0.0), axis=1, keepdims=True)

    squares = jnp.sum(stream * stream, axis=1, keepdims=True)
    mine = lax.broadcasted_iota(jnp.int32, (HR, rows), 0) + h * HR == lax.broadcasted_iota(
        jnp.int32, (HR, rows), 1
    )
    square_row = jnp.sum(jnp.where(mine, squares, 0.0), axis=0, keepdims=True)
    ss_send[...] = jnp.broadcast_to(square_row, (8, rows))
    for i in range(1, S):
        t = seq_peer(i)
        remote(ss_send, ss_r1.at[s], s1_ss.at[t], s1_rs.at[s], (t, h)).start()
    ss_r1[s] = ss_send[...]

    def squares_on():
        for i in range(1, S):
            t = seq_peer(i)
            remote(ss_send, ss_r1.at[t], s1_ss.at[t], s1_rs.at[t], (t, h)).wait_recv()
        part = ss_r1[0]
        for i in range(1, S):
            part = part + ss_r1[i]
        ss_mid[...] = part
        ss_r2[h] = part
        for i in range(1, H):
            t = head_peer(i)
            remote(ss_mid, ss_r2.at[h], s2_ss.at[t], s2_rs.at[h], (s, t)).start()

    for n in range(S + 2):
        if n + 1 < S:
            first_hop(n + 1)
        if n == 2:
            squares_on()
        if n < S:
            second_hop(n)
        if n >= 1 and n - 1 < S:
            product(n - 1)

    for i in range(1, H):
        t = head_peer(i)
        remote(ss_mid, ss_r2.at[t], s2_ss.at[t], s2_rs.at[t], (s, t)).wait_recv()
    square_sum = ss_r2[0, 0:1]
    for i in range(1, H):
        square_sum = square_sum + ss_r2[i, 0:1]
    inverse = to_col(lax.rsqrt(square_sum / D + epsilon))
    logits = acc[...] * inverse
    acc[...] = logits
    local_top = jnp.max(logits, axis=1, keepdims=True)
    local_sum = jnp.sum(jnp.exp(logits - local_top), axis=1, keepdims=True)
    ids = lax.broadcasted_iota(jnp.int32, (rows, VL), 1) + (s * H + h) * VL
    wanted = to_col(draft_ref[...].astype(f32)).astype(jnp.int32)
    picked = jnp.sum(jnp.where(ids == wanted, logits, 0.0), axis=1, keepdims=True)
    stat = [to_row(local_top), to_row(local_sum), to_row(picked)]

    def pack(stat):
        return jnp.concatenate(stat + [jnp.zeros((5, rows), f32)], axis=0)

    def merge(ref, count):
        top = ref[0, 0:1]
        for i in range(1, count):
            top = jnp.maximum(top, ref[i, 0:1])
        total = jnp.zeros((1, rows), f32)
        got = jnp.zeros((1, rows), f32)
        for i in range(count):
            total += ref[i, 1:2] * jnp.exp(ref[i, 0:1] - top)
            got += ref[i, 2:3]
        return [top, total, got]

    st_send[...] = pack(stat)
    for i in range(1, S):
        t = seq_peer(i)
        remote(st_send, st_r1.at[s], t1_ss.at[t], t1_rs.at[s], (t, h)).start()
    st_r1[s] = pack(stat)
    for b in range(B):
        for i in range(path_ref.shape[1]):
            path_out[b, i : i + 1, :] = acc[pl.ds(path_ref[b, i] + b * N, 1), :]
    for i in range(1, S):
        t = seq_peer(i)
        remote(st_send, st_r1.at[t], t1_ss.at[t], t1_rs.at[t], (t, h)).wait_recv()
    both = pack(merge(st_r1, S))
    st_mid[...] = both
    st_r2[h] = both
    for i in range(1, H):
        t = head_peer(i)
        remote(st_mid, st_r2.at[h], t2_ss.at[t], t2_rs.at[h], (s, t)).start()
    for i in range(1, H):
        t = head_peer(i)
        remote(st_mid, st_r2.at[t], t2_ss.at[t], t2_rs.at[t], (s, t)).wait_recv()
    top, total, got = merge(st_r2, H)
    logp_out[...] = got - (top + jnp.log(total))

    for i in range(1, S):
        t = seq_peer(i)
        remote(o_send.at[t], o_recv.at[s], o_ss.at[t], o_rs.at[s], (t, h)).wait_send()
        remote(ml_send.at[t], ml_recv.at[s], ml_ss.at[t], ml_rs.at[s], (t, h)).wait_send()
        remote(a_send, att_place(s), a_ss.at[t], a_rs.at[s], (t, h)).wait_send()
        remote(ss_send, ss_r1.at[s], s1_ss.at[t], s1_rs.at[s], (t, h)).wait_send()
        remote(st_send, st_r1.at[s], t1_ss.at[t], t1_rs.at[s], (t, h)).wait_send()
    for i in range(1, H):
        t = head_peer(i)
        remote(p_send.at[t], p_recv.at[h], p_ss.at[t], p_rs.at[h], (s, t)).wait_send()
        remote(ss_mid, ss_r2.at[h], s2_ss.at[t], s2_rs.at[h], (s, t)).wait_send()
        remote(st_mid, st_r2.at[h], t2_ss.at[t], t2_rs.at[h], (s, t)).wait_send()
    for c in sends:
        c.wait_send()


def on_device(
    S,
    H,
    queries,
    cache_keys,
    cache_values,
    new_keys,
    new_values,
    parents,
    path,
    lengths,
    draft_tokens,
    residual,
    out_weight,
    norm_gain,
    vocab_weight,
):
    B, heads, N, HD = queries.shape
    KV, keys = cache_keys.shape[1], cache_keys.shape[2]
    BK = B * KV
    R = B * heads * N // S
    rows = B * N
    DL = out_weight.shape[1]
    D, VL = vocab_weight.shape
    K = out_weight.shape[0]
    HR = rows // H
    HX = H // 2
    passes = (S // 2 - 1) + S // 2 + S * (HX - 1) + S + S * (HX - 1)
    vmem = pl.BlockSpec(memory_space=pltpu.VMEM)
    smem = pl.BlockSpec(memory_space=pltpu.SMEM)
    hbm = pl.BlockSpec(memory_space=pl.ANY)
    dma = pltpu.SemaphoreType.DMA
    path_logits, logp = pl.pallas_call(
        functools.partial(kernel, S, H, B, N, D),
        out_shape=(
            jax.ShapeDtypeStruct((B, path.shape[1], VL), f32),
            jax.ShapeDtypeStruct((1, rows), f32),
        ),
        in_specs=[smem, smem, vmem, vmem, vmem] + [hbm] * 8,
        out_specs=(vmem, vmem),
        scratch_shapes=[
            pltpu.VMEM((S, R, HD), bf16),
            pltpu.VMEM((BK, keys + N, HD), bf16),
            pltpu.VMEM((BK, keys + N, HD), bf16),
            pltpu.VMEM((rows, DL), bf16),
            pltpu.VMEM((K, DL), bf16),
            pltpu.VMEM((D, VL), bf16),
            pltpu.VMEM((B, N, R), f32),
            pltpu.VMEM((S, HD, R), bf16),
            pltpu.VMEM((S, 8, R), f32),
            pltpu.VMEM((S, HD, R), bf16),
            pltpu.VMEM((S, 8, R), f32),
            pltpu.VMEM((R // N, N, HD), bf16),
            pltpu.VMEM((heads, rows, HD), bf16),
            pltpu.VMEM((H, HR, DL), bf16),
            pltpu.VMEM((H, HR, DL), bf16),
            pltpu.VMEM((S, rows, DL), bf16),
            pltpu.VMEM((rows, VL), f32),
            pltpu.VMEM((8, rows), f32),
            pltpu.VMEM((S, 8, rows), f32),
            pltpu.VMEM((8, rows), f32),
            pltpu.VMEM((H, 8, rows), f32),
            pltpu.VMEM((8, rows), f32),
            pltpu.VMEM((S, 8, rows), f32),
            pltpu.VMEM((8, rows), f32),
            pltpu.VMEM((H, 8, rows), f32),
            dma((7,)),
            dma((S,)),
            dma((S,)), dma((S,)), dma((S,)), dma((S,)), dma((S,)), dma((S,)),
            dma((H,)), dma((H,)),
            dma((passes,)), dma((S * H,)),
            dma((S,)), dma((S,)), dma((H,)), dma((H,)),
            dma((S,)), dma((S,)), dma((H,)), dma((H,)),
        ],
        compiler_params=pltpu.CompilerParams(
            collective_id=0, has_side_effects=True, vmem_limit_bytes=62 * 1024 * 1024
        ),
        name="verify",
    )(
        lengths,
        path,
        parents,
        draft_tokens.reshape(1, rows),
        norm_gain.reshape(1, DL),
        queries.reshape(S, R, HD),
        cache_keys.reshape(BK, keys, HD),
        cache_values.reshape(BK, keys, HD),
        new_keys.reshape(BK, N, HD),
        new_values.reshape(BK, N, HD),
        residual.reshape(rows, DL),
        out_weight,
        vocab_weight,
    )
    return path_logits, logp.reshape(B, N)


def solution(mesh):
    placed = (
        P(None, "head", None, None),
        P(None, "head", "seq", None),
        P(None, "head", "seq", None),
        P(None, "head", None, None),
        P(None, "head", None, None),
        P(),
        P(),
        P(),
        P(),
        P(None, None, "seq"),
        P("head", "seq"),
        P("seq"),
        P(None, ("seq", "head")),
    )
    return jax.shard_map(
        functools.partial(on_device, mesh.shape["seq"], mesh.shape["head"]),
        mesh=mesh,
        in_specs=placed,
        out_specs=(P(None, None, ("seq", "head")), P()),
        check_vma=False,
    )
```

time: 350 us -> 83.8 us (0.24)
  blocking collectives: 184 us -> 0 us
  waiting for transfers between devices: 104 us -> 0 us
  Pallas kernels: 0 us -> 76.3 us
  matrix products: 27.8 us -> 0 us
  between operations: 14.6 us -> 0.64 us
  other arithmetic: 10.2 us -> 1.26 us
    pallas_call x0 -> x1, Pallas kernels: none -> 76.3 us  [on_device(): pl.pallas_call(functools.partial(kernel, S, H, B, N, D), out_shape=(jax.S...]
    pmax x2 -> x0, blocking collectives: 62.6 us -> none  [the longest x1 39.2 us: on_device(): vocab_top = lax.pmax(local_max, ('seq', 'head'))]
    psum x2 -> x0, blocking collectives: 61.3 us -> none  [the longest x1 40 us: on_device(): exp_sums, picked = lax.psum((local_sum, picked), ('seq', 'head'))]
    all_gather x1 -> x0, waiting for transfers between devices: 45.5 us -> none  [on_device(): portion = lax.all_gather(normed, 'seq', axis=2, tiled=True)]
    unnamed x1 -> x0, blocking collectives: 33.4 us -> none
    psum x1 -> x0, waiting for transfers between devices: 31.3 us -> none  [on_device(): projected = lax.psum(projected, 'head')]
    dot_general x14 -> x0, matrix products: 27.8 us -> none  [the longest x1 13.6 us: on_device(): jnp.dot(flat_part, vocab_weight, preferred_element_type=jnp.float32)]
    reduce_scatter x1 -> x0, waiting for transfers between devices: 27.2 us -> none  [on_device(): lax.psum_scatter(scaled, 'seq', scatter_dimension=2, tiled=True)]
  transfers between devices with their start and end apart: 3 -> 0, of which waited for: 3 -> 0; matrix products, arithmetic and copies ran while one was open for 0% -> 0% of each run, Pallas kernels for 0% -> 0%
where the time goes in v1:
time: 83.8 us; the launch traced here: 83.5 us
  Pallas kernels  76.3 us (91%)
  local copies, waits for them, and re-layouts  5.32 us (6%)
  other arithmetic  1.26 us (2%)
    pallas_call x1, Pallas kernels, on_device(): pl.pallas_call(functools.partial(kernel, S, H, B, N, D), out_shape=(jax.S...  76.3 us

profile of v1, /device:TPU:0, one launch (start us, length us, event | category | flops | bytes accessed | tf_op | source)
XLA Modules:
  0.0 83.5 jit_solution(9834967013638642032)
XLA Ops:
  0.6 1.3 %reshape.32.gain_ref = bf16[1,1024]{1,0:T(2,128)(2,1)} reshape(bf16[1024]{0:T(1024)(128)(2,1)} %param.24) | data formatting | bytes 4096 | tf_op jit(solution)/shard_map/reshape | solution.py:457
  1.9 1.3 %reshape.31.draft_ref = s32[1,128]{1,0:T(1,128)} reshape(s32[2,64]{1,0:T(2,128)} %param.21) | data formatting | bytes 1024 | tf_op jit(solution)/shard_map/reshape | solution.py:456
  3.2 76.3 %verify.1 = (f32[2,6,2048]{2,1,0:T(8,128)}, f32[1,128]{1,0:T(1,128)}) custom-call(s32[2]{0:T(128)} %len_ref.1, s32[2,6]{1,0:T(2,128)} %path_ref.1, s32[2,64]{1,0:T(2,128)} %par_ref.1, s32[1,128]{1,0:T(1,128)} %reshape.31.draft_ref, bf16[1,1024]{1,0:T(2,128)(2,1)} %reshape.32.gain_ref, bf16[8,256,128]{2,1,0:T(8,128)(2,1)} %bitcast.8, ...), custom_call_target="tpu_custom_call" | custom-call | tf_op jit(solution)/shard_map/verify/pallas_call | solution.py:406
  79.5 1.6 %copy.15 = f32[2,6,2048]{2,0,1:T(2,128)} copy(f32[2,6,2048]{2,1,0:T(8,128)} %get-tuple-element.6) | data formatting | bytes 196608
  81.1 0.5 broadcast.3
  81.6 1.3 %reduce.3 = f32[128]{0:T(128)S(1)} reduce(f32[1,128]{1,0:T(1,128)} %get-tuple-element.5, f32[]{:T(128)} %broadcast.3), dimensions={0}, to_apply=%get-tuple-element.5.reduce_sub_computation.3 | reduce | bytes 1028 | tf_op jit(solution)/shard_map/verify/pallas_call | solution.py:406
  82.9 0.6 reshape.39

commit v2 on v1

--- a/solution.py
+++ b/solution.py
@@ -13,6 +13,52 @@
 MESH = pl.DeviceIdType.MESH
 f32 = jnp.float32
 bf16 = jnp.bfloat16
+
+
+def route_steps(S, H):
+    names = []
+    for kind, count in (("z", S // 2), ("y", 2), ("x", H // 2), ("c", 2)):
+        while count > 1:
+            names.append((kind, count))
+            count //= 2
+    return names
+
+
+def subsets(names):
+    out = [frozenset()]
+    for n in names:
+        out += [c | {n} for c in out]
+    return out
+
+
+def last_step(offset, names):
+    return [n for n in names if n in offset][-1]
+
+
+def balanced(offset):
+    parts = {kind: sorted([n for n in offset if n[0] == kind], reverse=True) for kind in "zyxc"}
+    if parts["c"]:
+        return parts["c"][-1]
+    if parts["x"] and parts["y"]:
+        return parts["x"][-1] if len(parts["z"]) > 1 else parts["y"][-1]
+    if parts["x"]:
+        return parts["x"][-1]
+    if parts["y"]:
+        return parts["z"][-1] if len(parts["z"]) == 1 else parts["y"][-1]
+    return parts["z"][-1]
+
+
+def plan(names, via):
+    price = {n: 0.9 if n[0] == "c" else 1.6 + 0.75 * (min(n[1], 4) - 2) for n in names}
+    every = subsets(names)
+    cost = {frozenset(): 0.0}
+    for c in sorted(every, key=len):
+        if c:
+            n = via(c)
+            cost[c] = cost[c - {n}] + price[n] + 0.7
+    onward = {c: [n for n in names if n not in c and via(c | {n}) == n] for c in every}
+    rank = sorted(every, key=lambda c: (cost[c], sorted(c)))
+    return [(c, cost[c], onward[c]) for c in rank]
 
 
 def kernel(
@@ -66,14 +112,32 @@
     for i in range(1, H):
         pl.semaphore_signal(barrier, inc=1, device_id=(s, head_peer(i)), device_id_type=MESH)
 
-    Z = S // 2
-    y = lax.rem(s, 2)
-    z = s // 2
-    order = []
-    for i in range(Z):
-        zi = lax.rem(z + i, Z)
-        order.append(zi * 2 + y)
-        order.append(zi * 2 + (1 - y))
+    steps = route_steps(S, H)
+
+    def flip(value, span):
+        return 2 * (value // span * span) + span - 1 - value
+
+    def at_offset(offset):
+        zi, yi, xi, ci = s // 2, lax.rem(s, 2), h // 2, lax.rem(h, 2)
+        for name in offset:
+            kind, span = name
+            if kind == "z":
+                zi = flip(zi, span)
+            elif kind == "y":
+                yi = 1 - yi
+            elif kind == "x":
+                xi = flip(xi, span)
+            else:
+                ci = 1 - ci
+        return zi * 2 + yi, xi * 2 + ci
+
+    zy = [n for n in steps if n[0] in "zy"]
+    row_plan = plan(steps, balanced)
+    att_plan = plan(zy, lambda c: last_step(c, zy))
+    row_cost = {c: cost for c, cost, _ in row_plan}
+    xc = subsets([n for n in steps if n[0] in "xc"])
+    slabs = sorted(subsets(zy), key=lambda c: (max(row_cost[c | o] for o in xc), sorted(c)))
+    order = [at_offset(c)[0] for c in slabs]
 
     def slab(idx):
         return pl.ds(pl.multiple_of(idx * DL, DL), DL)
@@ -171,19 +235,24 @@
         return x_att.at[pl.ds(h0, heads_chunk), pl.ds(pl.multiple_of(t // group * N, N), N), :]
 
     a_send[...] = att
-    for i in range(1, S):
-        t = seq_peer(i)
-        remote(a_send, att_place(s), a_ss.at[t], a_rs.at[s], (t, h)).start()
     x_att[
         pl.ds(lax.rem(s, group) * heads_chunk, heads_chunk),
         pl.ds(pl.multiple_of(s // group * N, N), N),
         :,
     ] = att
+    a_sends = []
+    for c, _, onward in att_plan:
+        si = at_offset(c)[0]
+        if c:
+            remote(att_place(si), att_place(si), a_ss.at[0], a_rs.at[si], (s, h)).wait_recv()
+        for n in onward:
+            src = att_place(si) if c else a_send
+            to = at_offset([n])[0]
+            copy = remote(src, att_place(si), a_ss.at[len(a_sends)], a_rs.at[si], (to, h))
+            copy.start()
+            a_sends.append(copy)
     loads[5].wait()
     loads[6].wait()
-    for i in range(1, S):
-        t = seq_peer(i)
-        remote(a_send, att_place(t), a_ss.at[t], a_rs.at[t], (t, h)).wait_recv()
 
     lhs = jnp.concatenate([x_att[i] for i in range(x_att.shape[0])], axis=1)
     proj = jnp.dot(lhs, ow[...], preferred_element_type=f32)
@@ -198,7 +267,7 @@
         t = head_peer(i)
         remote(p_send.at[t], p_recv.at[t], p_ss.at[t], p_rs.at[t], (s, t)).wait_recv()
         stream += p_recv[t].astype(f32)
-    g[s, my_rows, :] = (stream * gain_ref[...].astype(f32)).astype(bf16)
+    g[s, my_rows, :] = (stream * gain_ref[...].astype(f32)[None, :]).astype(bf16)
 
     def block(si, hi):
         return g.at[si, pl.ds(pl.multiple_of(hi * HR, HR), HR), :]
@@ -213,38 +282,17 @@
     def arrive(si, hi):
         remote(block(si, hi), block(si, hi), g_ss.at[0], g_rs.at[si * H + hi], (s, h)).wait_recv()
 
-    HX = H // 2
-    hx, hc = h // 2, lax.rem(h, 2)
-    partner = hx * 2 + (1 - hc)
-    far = [lax.rem(hx + i, HX) * 2 + hc for i in range(1, HX)]
-    far_partner = [lax.rem(hx + i, HX) * 2 + (1 - hc) for i in range(1, HX)]
-    y_dev = z * 2 + (1 - y)
-
-    def first_hop(n):
-        si = order[n]
-        if n == 0:
-            for i in range(1, Z):
-                pass_on(si, h, (order[2 * i], h))
-        else:
-            arrive(si, h)
-        if n % 2 == 0:
-            pass_on(si, h, (y_dev, h))
-        for t in far:
-            pass_on(si, h, (s, t))
-        pass_on(si, h, (s, partner))
-
-    def second_hop(n):
-        for t in far:
-            arrive(order[n], t)
-            pass_on(order[n], t, (s, partner))
+    def event(c, onward):
+        si, hi = at_offset(c)
+        if c:
+            arrive(si, hi)
+        for n in onward:
+            pass_on(si, hi, at_offset([n]))
 
     tiles = max(1, VL // 512)
     width = VL // tiles
 
     def product(n):
-        arrive(order[n], partner)
-        for t in far_partner:
-            arrive(order[n], t)
         vw_copy(n).wait()
         left = g[order[n]]
 
@@ -256,7 +304,7 @@
 
         lax.fori_loop(0, tiles, tile, 0)
 
-    first_hop(0)
+    event(*row_plan[0][::2])
 
     eye = lax.broadcasted_iota(jnp.int32, (rows, rows), 0) == lax.broadcasted_iota(
         jnp.int32, (rows, rows), 1
@@ -292,15 +340,18 @@
             t = head_peer(i)
             remote(ss_mid, ss_r2.at[h], s2_ss.at[t], s2_rs.at[h], (s, t)).start()
 
-    for n in range(S + 2):
-        if n + 1 < S:
-            first_hop(n + 1)
-        if n == 2:
+    place = {c: n for n, (c, _, _) in enumerate(row_plan)}
+    ready = [max(place[c | o] for o in xc) for c in slabs]
+    done = 0
+    for n in range(1, S * H):
+        event(*row_plan[n][::2])
+        if n == S * H // 4:
             squares_on()
-        if n < S:
-            second_hop(n)
-        if n >= 1 and n - 1 < S:
-            product(n - 1)
+        while done < S and ready[done] + 2 <= n:
+            product(done)
+            done += 1
+    for n in range(done, S):
+        product(n)
 
     for i in range(1, H):
         t = head_peer(i)
@@ -314,7 +365,8 @@
     local_top = jnp.max(logits, axis=1, keepdims=True)
     local_sum = jnp.sum(jnp.exp(logits - local_top), axis=1, keepdims=True)
     ids = lax.broadcasted_iota(jnp.int32, (rows, VL), 1) + (s * H + h) * VL
-    wanted = to_col(draft_ref[...].astype(f32)).astype(jnp.int32)
+    drafts = jnp.concatenate([draft_ref[b : b + 1, :] for b in range(B)], axis=1)
+    wanted = to_col(drafts.astype(f32)).astype(jnp.int32)
     picked = jnp.sum(jnp.where(ids == wanted, logits, 0.0), axis=1, keepdims=True)
     stat = [to_row(local_top), to_row(local_sum), to_row(picked)]
 
@@ -353,13 +405,14 @@
         t = head_peer(i)
         remote(st_mid, st_r2.at[t], t2_ss.at[t], t2_rs.at[t], (s, t)).wait_recv()
     top, total, got = merge(st_r2, H)
-    logp_out[...] = got - (top + jnp.log(total))
+    logp = got - (top + jnp.log(total))
+    for b in range(B):
+        logp_out[b : b + 1, :] = logp[:, b * N : (b + 1) * N]
 
     for i in range(1, S):
         t = seq_peer(i)
         remote(o_send.at[t], o_recv.at[s], o_ss.at[t], o_rs.at[s], (t, h)).wait_send()
         remote(ml_send.at[t], ml_recv.at[s], ml_ss.at[t], ml_rs.at[s], (t, h)).wait_send()
-        remote(a_send, att_place(s), a_ss.at[t], a_rs.at[s], (t, h)).wait_send()
         remote(ss_send, ss_r1.at[s], s1_ss.at[t], s1_rs.at[s], (t, h)).wait_send()
         remote(st_send, st_r1.at[s], t1_ss.at[t], t1_rs.at[s], (t, h)).wait_send()
     for i in range(1, H):
@@ -367,7 +420,7 @@
         remote(p_send.at[t], p_recv.at[h], p_ss.at[t], p_rs.at[h], (s, t)).wait_send()
         remote(ss_mid, ss_r2.at[h], s2_ss.at[t], s2_rs.at[h], (s, t)).wait_send()
         remote(st_mid, st_r2.at[h], t2_ss.at[t], t2_rs.at[h], (s, t)).wait_send()
-    for c in sends:
+    for c in a_sends + sends:
         c.wait_send()
 
 
@@ -397,8 +450,7 @@
     D, VL = vocab_weight.shape
     K = out_weight.shape[0]
     HR = rows // H
-    HX = H // 2
-    passes = (S // 2 - 1) + S // 2 + S * (HX - 1) + S + S * (HX - 1)
+    passes = S * H - 1
     vmem = pl.BlockSpec(memory_space=pltpu.VMEM)
     smem = pl.BlockSpec(memory_space=pltpu.SMEM)
     hbm = pl.BlockSpec(memory_space=pl.ANY)
@@ -407,7 +459,7 @@
         functools.partial(kernel, S, H, B, N, D),
         out_shape=(
             jax.ShapeDtypeStruct((B, path.shape[1], VL), f32),
-            jax.ShapeDtypeStruct((1, rows), f32),
+            jax.ShapeDtypeStruct((B, N), f32),
         ),
         in_specs=[smem, smem, vmem, vmem, vmem] + [hbm] * 8,
         out_specs=(vmem, vmem),
@@ -453,8 +505,8 @@
         lengths,
         path,
         parents,
-        draft_tokens.reshape(1, rows),
-        norm_gain.reshape(1, DL),
+        draft_tokens,
+        norm_gain,
         queries.reshape(S, R, HD),
         cache_keys.reshape(BK, keys, HD),
         cache_values.reshape(BK, keys, HD),
@@ -464,7 +516,7 @@
         out_weight,
         vocab_weight,
     )
-    return path_logits, logp.reshape(B, N)
+    return path_logits, logp
 
 
 def solution(mesh):

time: 83.8 us -> 75.3 us (0.90)
  Pallas kernels: 76.3 us -> 71.7 us
  local copies, waits for them, and re-layouts: 5.32 us -> 2.85 us
  other arithmetic: 1.26 us -> 0 us
    pallas_call x1, Pallas kernels: 76.3 us -> 71.7 us  [on_device(): pl.pallas_call(functools.partial(kernel, S, H, B, N, D), out_shape=(jax.S...]
    reshape x3 -> x0, local copies, waits for them, and re-layouts: 3.19 us -> none  [the longest x1 1.28 us: on_device(): norm_gain.reshape(1, DL)]
    pallas_call x1 -> x0, other arithmetic: 1.26 us -> none  [on_device(): pl.pallas_call(functools.partial(kernel, S, H, B, N, D), out_shape=(jax.S...]
    pallas_call x1, local copies, waits for them, and re-layouts: 0.51 us -> 1.62 us  [on_device(): pl.pallas_call(functools.partial(kernel, S, H, B, N, D), out_shape=(jax.S...]
where the time goes in v2:
time: 75.3 us; the launch traced here: 75.2 us
  Pallas kernels  71.7 us (95%)
  local copies, waits for them, and re-layouts  2.85 us (4%)
    pallas_call x1, Pallas kernels, on_device(): pl.pallas_call(functools.partial(kernel, S, H, B, N, D), out_shape=(jax.S...  71.7 us
    pallas_call x1, local copies, waits for them, and re-layouts, on_device(): pl.pallas_call(functools.partial(kernel, S, H, B, N, D), out_shape=(jax.S...  1.62 us

profile of v2, /device:TPU:0, one launch (start us, length us, event | category | flops | bytes accessed | tf_op | source)
XLA Modules:
  0.0 75.2 jit_solution(4836351261546465093)
XLA Ops:
  0.6 71.7 %verify.1 = (f32[2,6,2048]{2,1,0:T(8,128)}, f32[2,64]{1,0:T(2,128)}) custom-call(s32[2]{0:T(128)} %len_ref.1, s32[2,6]{1,0:T(2,128)} %path_ref.1, s32[2,64]{1,0:T(2,128)} %par_ref.1, s32[2,64]{1,0:T(2,128)} %draft_ref.1, bf16[1024]{0:T(1024)(128)(2,1)} %gain_ref.1, bf16[8,256,128]{2,1,0:T(8,128)(2,1)} %bitcast.8, bf16[4,1024,128]{2,1,0:T(8,128)(2,1)} %bitcast.6, ...), custom_call_target="tpu_custom_call" | custom-call | tf_op jit(solution)/shard_map/verify/pallas_call | solution.py:458
  72.3 1.6 %copy.15 = f32[2,6,2048]{2,0,1:T(2,128)} copy(f32[2,6,2048]{2,1,0:T(8,128)} %get-tuple-element.2) | data formatting | bytes 196608 | tf_op jit(solution)/shard_map/verify/pallas_call | solution.py:458
  73.9 1.2 %copy.17 = f32[2,64]{1,0:T(2,128)} copy(f32[2,64]{1,0:T(2,128)} %get-tuple-element.7) | data formatting | bytes 1024
